TPU v7x, 32 devices: a whole 2x2x4 slice. The times are simulated.
32 devices in a mesh: groups: 2 (over x), frame: 8 (over z, y), space: 2 (over core).
Axes of the slice: x: 2, y: 2, z: 4, core: 2. Of those that a mesh axis runs over, the one named last changes fastest.
Arguments:
- queries: bfloat16 [16, 12, 80, 2240], P(('groups', 'frame'), 'space'), parts along dimension 0, may hold values from -6 to 6
- keys: bfloat16 [16, 12, 80, 2240], P(('groups', 'frame'), 'space'), parts along dimension 0, may hold values from -6 to 6
- values: bfloat16 [16, 12, 80, 2240], P(('groups', 'frame'), 'space'), parts along dimension 0, may hold values from -6 to 6
- residual: bfloat16 [16, 12, 80, 2240], P(('groups', 'frame'), 'space'), parts along dimension 0, may hold values from -6 to 6
- attn_gain: float32 [2240], replicated, may hold values from 0.5 to 1.5
- value_taps: float32 [9, 2240], replicated, may hold values from -2 to 2
- gate_taps: float32 [9, 2240], replicated, may hold values from -2 to 2
Outputs:
- block_out: bfloat16 [16, 12, 80, 2240], P(('groups', 'frame'), 'space'), parts along dimension 0
There are 2 independent parts, one for each index of `groups`. A program takes and returns all parts, laid end to end along the dimension named above; an argument that names none is the same for every part. Nothing has to cross between parts.
All inputs are finite; a program needn't handle non-finite values.
Results may differ from a plain program's by a relative error of at most 0.008.
Values may be sent and summed in bfloat16 or wider, within the bound.
A program may use at most 128 MiB of HBM per device.

v0:
```python
import functools

import jax
import jax.numpy as jnp
from jax import lax
from jax.experimental import pallas as pl
from jax.experimental.pallas import tpu as pltpu
from jax.sharding import PartitionSpec as P

HEAD_DIM = 112
LANES = 128
WINDOW = 256
PAD = 8
PIECE = 768
BLOCK = 384
LAG = 2
AHEAD = 2
F32, BF16 = jnp.float32, jnp.bfloat16


def windows(dim):
    out = []
    for lo in range(0, dim, WINDOW):
        w = min(WINDOW, dim - lo)
        h0, h1 = lo // HEAD_DIM, (lo + w - 1) // HEAD_DIM
        ks = HEAD_DIM * h0 // LANES * LANES
        ke = min(dim, -(-HEAD_DIM * (h1 + 1) // LANES) * LANES)
        out.append((lo, w, range(h0, h1 + 1), ks, ke))
    return out


def mix_kernel(
    frames, rows, width, dim,
    q_hbm, k_hbm, v_hbm, r_hbm, gain_ref, o_hbm,
    q, k, v, res, st, pb, rb, ob, yb, pr, ps, vb, numer, sq, mixed,
    kv_sem, load_sem, edge_s, edge_r, rs_s, rs_r, ag_s, ag_r, y_s, y_r, z_s, z_r, pv_s, pv_r, out_sem,
):
    tokens = rows * width
    tiles = st.shape[0]
    space = lax.axis_index("space")
    frame = lax.axis_index("frame")
    other = 1 - space
    pair, odd = frame // 2, frame % 2
    twin = frame + 1 - 2 * odd
    has_prev = pair > 0
    has_next = pair < frames // 2 - 1
    wins = windows(dim)
    steps = len(wins)

    cuts = list(range(0, dim, PIECE)) + [dim]
    kv_loads = []
    for i, (lo, hi) in enumerate(zip(cuts, cuts[1:])):
        kv_loads.append(
            [
                pltpu.make_async_copy(src.at[:, lo:hi], dst.at[:, lo:hi], kv_sem.at[c, i])
                for c, (src, dst) in enumerate(((k_hbm, k), (v_hbm, v)))
            ]
        )
    loads = [
        pltpu.make_async_copy(src, dst.at[0:tokens], load_sem.at[i]) for i, (src, dst) in enumerate(((q_hbm, q), (r_hbm, res)))
    ]
    for copies in kv_loads:
        for copy in copies:
            copy.start()
    for copy in loads:
        copy.start()

    barrier = pltpu.get_barrier_semaphore()
    pl.semaphore_signal(barrier, inc=1, device_id={"space": other})
    pl.semaphore_signal(barrier, inc=1, device_id={"frame": twin})

    @pl.when(has_prev)
    def _():
        pl.semaphore_signal(barrier, inc=1, device_id={"frame": frame - 2})

    @pl.when(has_next)
    def _():
        pl.semaphore_signal(barrier, inc=1, device_id={"frame": frame + 2})

    st[tiles - 1] = jnp.zeros(st.shape[1:], F32)
    mixed[pl.ds(pl.multiple_of(space * (tokens + width), width), width), :] = jnp.zeros((width, dim), BF16)

    pl.semaphore_wait(barrier, 2 + jnp.where(has_prev, 1, 0) + jnp.where(has_next, 1, 0))

    def to_other(src, dst, tile, send, recv, j):
        return pltpu.make_async_remote_copy(
            src_ref=src.at[tile], dst_ref=dst.at[tile], send_sem=send.at[j], recv_sem=recv.at[j],
            device_id={"space": other},
        )

    def to_frame(src, dst, tile, send, recv, j, target):
        return pltpu.make_async_remote_copy(
            src_ref=src.at[tile], dst_ref=dst.at[tile], send_sem=send.at[j], recv_sem=recv.at[j],
            device_id={"frame": target},
        )

    edges = [
        pltpu.make_async_remote_copy(
            src_ref=src.at[pl.ds(pl.multiple_of(other * (tokens - width), width), width)],
            dst_ref=dst.at[tokens : tokens + width],
            send_sem=edge_s.at[i], recv_sem=edge_r.at[i], device_id={"space": other},
        )
        for i, (src, dst) in enumerate(((q_hbm, q), (r_hbm, res)))
    ]

    def head_of(lo, w):
        return (lax.broadcasted_iota(jnp.int32, (HEAD_DIM, w), 1) + lo) // HEAD_DIM

    def own_step(j):
        tile = 2 * j + space
        to_other(pb, rb, tile, rs_s, rs_r, j).wait_recv()
        total = st[tile] + rb[tile].astype(F32)
        st[tile] = total
        ob[tile] = total.astype(BF16)
        to_frame(ob, yb, tile, y_s, y_r, j, twin).start()
        to_other(ob, ob, tile, ag_s, ag_r, j).start()

    ready = 0
    for m in range(steps):
        lo, w, heads, ks, ke = wins[m]
        while cuts[ready] < ke:
            for copy in kv_loads[ready]:
                copy.wait()
            ready += 1
        full = lax.dot_general(
            jnp.maximum(k[:, ks:ke], 0), v[:, lo : lo + w], (((0,), (0,)), ((), ())), preferred_element_type=F32
        )
        owner = head_of(lo, w)
        slab = jnp.zeros((HEAD_DIM, w), F32)
        for h in heads:
            at = HEAD_DIM * h - ks
            slab = jnp.where(owner == h, full[at : at + HEAD_DIM, :], slab)
        for part in range(-(-w // LANES)):
            tile = lo // LANES + part
            wide = min(LANES, w - part * LANES)
            st[tile, :, :wide] = slab[:, part * LANES : part * LANES + wide]
            pb[tile] = st[tile].astype(BF16)
        to_other(pb, rb, 2 * m + other, rs_s, rs_r, m).start()
        if m >= LAG:
            own_step(m - LAG)
    for m in range(max(0, steps - LAG), steps):
        own_step(m)
    for copy in edges:
        copy.start()

    def scan_step(j):
        tile = 2 * j + space
        to_frame(ob, yb, tile, y_s, y_r, j, twin).wait_recv()
        beside = yb[tile].astype(F32)

        @pl.when(has_prev)
        def _():
            to_frame(ps, pr, tile, z_s, z_r, j, frame - 2).wait_recv()

        @pl.when(jnp.logical_not(has_prev))
        def _():
            pr[tile] = jnp.zeros(pr.shape[1:], BF16)

        before = pr[tile].astype(F32)

        @pl.when(has_next)
        def _():
            ps[tile] = (before + (st[tile] + beside)).astype(BF16)
            to_frame(ps, pr, tile, z_s, z_r, j, frame + 2).start()

        vb[tile] = (before + beside * odd.astype(F32)).astype(BF16)
        to_other(vb, vb, tile, pv_s, pv_r, j).start()

    @pl.when(has_next)
    def _():
        def relay(j, _):
            scan_step(j)
            return 0

        lax.fori_loop(0, steps, relay, 0)

    def last_in_chain(first, end):
        @pl.when(jnp.logical_not(has_next))
        def _():
            for j in range(first, min(end, steps)):
                scan_step(j)

    def spread(state, lo, w, heads, ks, ke):
        first = lo // LANES
        slab = jnp.concatenate([state[first + p] for p in range(-(-w // LANES))], axis=1)[:, :w]
        owner = head_of(lo, w)
        pieces = []
        if HEAD_DIM * heads[0] > ks:
            pieces.append(jnp.zeros((HEAD_DIM * heads[0] - ks, w), BF16))
        for h in heads:
            pieces.append(jnp.where(owner == h, slab, jnp.zeros_like(slab)))
        end = HEAD_DIM * (heads[-1] + 1)
        if end < ke:
            pieces.append(jnp.zeros((ke - end, w), BF16))
        return jnp.concatenate(pieces, axis=0)

    for copy in loads:
        copy.wait()
    for copy in edges:
        copy.wait_recv()

    def numer_step(m):
        lo, w, heads, ks, ke = wins[m]
        tile = 2 * m + other
        to_other(ob, ob, tile, ag_s, ag_r, m).wait_recv()
        to_other(vb, vb, tile, pv_s, pv_r, m).wait_recv()
        phi = jnp.maximum(q[:, ks:ke], 0)
        found = jnp.dot(phi, spread(vb, lo, w, heads, ks, ke), preferred_element_type=F32)
        found = found + jnp.dot(phi, spread(ob, lo, w, heads, ks, ke), preferred_element_type=F32)
        numer[:, lo : lo + w] = found
        sq[:, lo : lo + w] = (found * found).astype(BF16)

    far = pl.ds(pl.multiple_of((1 - space) * (tokens + width), width), width)
    stores = []

    def mixed_step(m):
        lo, w, heads, ks, ke = wins[m]
        from_head = (lax.broadcasted_iota(jnp.int32, (ke - ks, w), 0) + ks) // HEAD_DIM
        to_head = (lax.broadcasted_iota(jnp.int32, (ke - ks, w), 1) + lo) // HEAD_DIM
        same = jnp.where(from_head == to_head, 1.0, 0.0).astype(BF16)
        total = jnp.dot(sq[:, ks:ke], same, preferred_element_type=F32)
        scale = lax.rsqrt(total * (1.0 / HEAD_DIM) + 1e-6)
        normed = numer[:, lo : lo + w] * scale
        value = (res[:, lo : lo + w].astype(F32) + normed * gain_ref[lo : lo + w].reshape(1, w)).astype(BF16)
        mixed[width : width + tokens, lo : lo + w] = value[:tokens]
        mixed[far, lo : lo + w] = value[tokens:]
        store = pltpu.make_async_copy(mixed.at[:, lo : lo + w], o_hbm.at[:, lo : lo + w], out_sem.at[m])
        store.start()
        stores.append(store)

    last_in_chain(0, AHEAD)
    for m in range(steps):
        last_in_chain(m + AHEAD, m + AHEAD + 1)
        numer_step(m)
        if m > 0:
            mixed_step(m - 1)
    mixed_step(steps - 1)

    for copy in edges:
        copy.wait_send()

    def drain_step(j, _):
        mine, theirs = 2 * j + space, 2 * j + other
        to_other(pb, rb, theirs, rs_s, rs_r, j).wait_send()
        to_other(ob, ob, mine, ag_s, ag_r, j).wait_send()
        to_frame(ob, yb, mine, y_s, y_r, j, twin).wait_send()
        to_other(vb, vb, mine, pv_s, pv_r, j).wait_send()

        @pl.when(has_next)
        def _():
            to_frame(ps, pr, mine, z_s, z_r, j, frame + 2).wait_send()

        return 0

    lax.fori_loop(0, steps, drain_step, 0)
    for store in stores:
        store.wait()


def conv_kernel(rows, width, m_ref, vt_ref, gt_ref, o_ref, x32):
    step = width + 2 * PAD
    part = 16

    @pl.when(pl.program_id(0) == 0)
    def _():
        x32[...] = jnp.zeros_like(x32)

    def tile_step(t, _):
        at = pl.ds(pl.multiple_of(t * LANES, LANES), LANES)
        for row in range(rows + 2):
            x32[row * step + PAD : row * step + PAD + width, :] = m_ref[row * width : (row + 1) * width, at].astype(F32)
        taps = [
            (jnp.broadcast_to(vt_ref[n : n + 1, at], (part, LANES)), jnp.broadcast_to(gt_ref[n : n + 1, at], (part, LANES)))
            for n in range(9)
        ]
        for row in range(rows):
            for off in range(0, width, part):
                cv, cg = None, None
                for n in range(9):
                    start = (row + n // 3) * step + PAD - 1 + n % 3 + off
                    x = x32[start : start + part, :]
                    cv = taps[n][0] * x if cv is None else cv + taps[n][0] * x
                    cg = taps[n][1] * x if cg is None else cg + taps[n][1] * x
                centre = (row + 1) * step + PAD + off
                half = 0.5 * cg
                value = x32[centre : centre + part, :] + cv * (half + half * jnp.tanh(half))
                o_ref[row * width + off : row * width + off + part, at] = value.astype(BF16)
        return 0

    lax.fori_loop(0, o_ref.shape[1] // LANES, tile_step, 0)


def solution(mesh):
    frames = mesh.shape["frame"]

    def on_device(queries, keys, values, residual, attn_gain, value_taps, gate_taps):
        _, rows, width, dim = queries.shape
        tokens = rows * width
        steps = -(-dim // WINDOW)
        flat = lambda a: a.reshape(tokens, dim)
        anywhere = pl.BlockSpec(memory_space=pl.ANY)
        state = (2 * steps, HEAD_DIM, LANES)
        sems = pltpu.SemaphoreType.DMA((steps,))
        two = pltpu.SemaphoreType.DMA((2,))
        ext = tokens + width
        mixed = pl.pallas_call(
            functools.partial(mix_kernel, frames, rows, width, dim),
            out_shape=jax.ShapeDtypeStruct((tokens + 2 * width, dim), BF16),
            in_specs=[anywhere] * 4 + [pl.BlockSpec(memory_space=pltpu.VMEM)],
            out_specs=anywhere,
            scratch_shapes=[
                pltpu.VMEM((ext, dim), BF16),
                pltpu.VMEM((tokens, dim), BF16),
                pltpu.VMEM((tokens, dim), BF16),
                pltpu.VMEM((ext, dim), BF16),
                pltpu.VMEM(state, F32),
            ]
            + [pltpu.VMEM(state, BF16)] * 7
            + [
                pltpu.VMEM((ext, dim), F32),
                pltpu.VMEM((ext, dim), BF16),
                pltpu.VMEM((tokens + 2 * width, dim), BF16),
                pltpu.SemaphoreType.DMA((2, -(-dim // PIECE))),
                two,
                two,
                two,
            ]
            + [sems] * 11,
            compiler_params=pltpu.CompilerParams(collective_id=0, has_side_effects=True, vmem_limit_bytes=56 << 20),
        )(flat(queries), flat(keys), flat(values), flat(residual), attn_gain, )
        out = pl.pallas_call(
            functools.partial(conv_kernel, rows, width),
            out_shape=jax.ShapeDtypeStruct((tokens, dim), BF16),
            grid=(-(-dim // BLOCK),),
            in_specs=[
                pl.BlockSpec((tokens + 2 * width, BLOCK), lambda c: (0, c)),
                pl.BlockSpec((9, BLOCK), lambda c: (0, c)),
                pl.BlockSpec((9, BLOCK), lambda c: (0, c)),
            ],
            out_specs=pl.BlockSpec((tokens, BLOCK), lambda c: (0, c)),
            scratch_shapes=[pltpu.VMEM(((rows + 2) * (width + 2 * PAD), LANES), F32)],
        )(mixed, value_taps, gate_taps)
        return out.reshape(1, rows, width, dim)

    placed = P(("groups", "frame"), "space", None, None)
    return jax.shard_map(
        on_device,
        mesh=mesh,
        in_specs=(placed,) * 4 + (P(),) * 3,
        out_specs=placed,
        check_vma=False,
    )
```

profile of v0, /device:TPU:27, one launch (start us, length us, event | category | flops | bytes accessed | tf_op | source)
XLA Modules:
  0.0 35.1 jit_solution(16892526458199071350)
XLA Ops:
  0.0 26.4 %shard_map.73.m_ref = bf16[640,2240]{1,0:T(8,128)(2,1)} custom-call(bf16[480,2240]{1,0:T(8,128)(2,1)} %bitcast.5, bf16[480,2240]{1,0:T(8,128)(2,1)} %bitcast.6, bf16[480,2240]{1,0:T(8,128)(2,1)} %bitcast.7, bf16[480,2240]{1,0:T(8,128)(2,1)} %bitcast.8, f32[2240]{0:T(1024)} %gain_ref.1), custom_call_target="tpu_custom_call" | custom-call | tf_op jit(solution)/shard_map/pallas_call | solution.py:306
  26.4 8.7 %shard_map.74 = bf16[480,2240]{1,0:T(8,128)(2,1)} custom-call(bf16[640,2240]{1,0:T(8,128)(2,1)} %shard_map.73.m_ref, f32[9,2240]{1,0:T(8,128)} %vt_ref.1, f32[9,2240]{1,0:T(8,128)} %gt_ref.1), custom_call_target="tpu_custom_call" | custom-call | tf_op jit(solution)/shard_map/pallas_call | solution.py:331
where the time goes:
time: 35.7 us; the launch traced here: 35.1 us
  Pallas kernels  35.1 us (98%)
    pallas_call x1, Pallas kernels, on_device(): pl.pallas_call(functools.partial(mix_kernel, frames, rows, width, dim), o...  26.4 us
    pallas_call x1, Pallas kernels, on_device(): pl.pallas_call(functools.partial(conv_kernel, rows, width), out_shape=jax...  8.69 us

commit v1 on v0

--- a/solution.py
+++ b/solution.py
@@ -11,9 +11,10 @@
 LANES = 128
 WINDOW = 256
 PAD = 8
-PIECE = 768
+PIECE = 384
 BLOCK = 384
-LAG = 2
+PAIR = 2 * HEAD_DIM
+LAG = 4
 AHEAD = 2
 F32, BF16 = jnp.float32, jnp.bfloat16
 
@@ -32,8 +33,8 @@
 def mix_kernel(
     frames, rows, width, dim,
     q_hbm, k_hbm, v_hbm, r_hbm, gain_ref, o_hbm,
-    q, k, v, res, st, pb, rb, ob, yb, pr, ps, vb, numer, sq, mixed,
-    kv_sem, load_sem, edge_s, edge_r, rs_s, rs_r, ag_s, ag_r, y_s, y_r, z_s, z_r, pv_s, pv_r, out_sem,
+    q, k, v, res, st, pb, rb, ob, yb, pr, ps, vb, qa, ra, ga, numer, sq, mixed,
+    kv_sem, load_sem, edge_s, edge_r, rs_s, rs_r, y_s, y_r, z_s, z_r, pv_s, pv_r, out_sem,
 ):
     tokens = rows * width
     tiles = st.shape[0]
@@ -62,8 +63,6 @@
     for copies in kv_loads:
         for copy in copies:
             copy.start()
-    for copy in loads:
-        copy.start()
 
     barrier = pltpu.get_barrier_semaphore()
     pl.semaphore_signal(barrier, inc=1, device_id={"space": other})
@@ -113,7 +112,6 @@
         st[tile] = total
         ob[tile] = total.astype(BF16)
         to_frame(ob, yb, tile, y_s, y_r, j, twin).start()
-        to_other(ob, ob, tile, ag_s, ag_r, j).start()
 
     ready = 0
     for m in range(steps):
@@ -122,6 +120,9 @@
             for copy in kv_loads[ready]:
                 copy.wait()
             ready += 1
+            if ready == len(kv_loads):
+                for copy in loads:
+                    copy.start()
         full = lax.dot_general(
             jnp.maximum(k[:, ks:ke], 0), v[:, lo : lo + w], (((0,), (0,)), ((), ())), preferred_element_type=F32
         )
@@ -163,78 +164,86 @@
             ps[tile] = (before + (st[tile] + beside)).astype(BF16)
             to_frame(ps, pr, tile, z_s, z_r, j, frame + 2).start()
 
-        vb[tile] = (before + beside * odd.astype(F32)).astype(BF16)
+        vb[tile] = (before + beside * odd.astype(F32) + st[tile]).astype(BF16)
         to_other(vb, vb, tile, pv_s, pv_r, j).start()
 
-    @pl.when(has_next)
-    def _():
-        def relay(j, _):
-            scan_step(j)
-            return 0
-
-        lax.fori_loop(0, steps, relay, 0)
-
-    def last_in_chain(first, end):
-        @pl.when(jnp.logical_not(has_next))
-        def _():
-            for j in range(first, min(end, steps)):
-                scan_step(j)
-
-    def spread(state, lo, w, heads, ks, ke):
-        first = lo // LANES
-        slab = jnp.concatenate([state[first + p] for p in range(-(-w // LANES))], axis=1)[:, :w]
-        owner = head_of(lo, w)
-        pieces = []
-        if HEAD_DIM * heads[0] > ks:
-            pieces.append(jnp.zeros((HEAD_DIM * heads[0] - ks, w), BF16))
-        for h in heads:
-            pieces.append(jnp.where(owner == h, slab, jnp.zeros_like(slab)))
-        end = HEAD_DIM * (heads[-1] + 1)
-        if end < ke:
-            pieces.append(jnp.zeros((ke - end, w), BF16))
-        return jnp.concatenate(pieces, axis=0)
+    pairs = dim // PAIR
+
+    def realign(r0, r1):
+        for j in range(pairs):
+            qa[j, r0:r1, :PAIR] = jnp.maximum(q[r0:r1, PAIR * j : PAIR * (j + 1)], 0)
+            ra[j, r0:r1, :PAIR] = res[r0:r1, PAIR * j : PAIR * (j + 1)]
+
+    def cover(lo, hi, size):
+        out = []
+        while lo < hi:
+            n = lo // size
+            top = min(hi, size * (n + 1))
+            out.append((n, lo - size * n, top - size * n))
+            lo = top
+        return out
+
+    row_head = lax.broadcasted_iota(jnp.int32, (PAIR, PAIR), 0) < HEAD_DIM
+    col_head = lax.broadcasted_iota(jnp.int32, (PAIR, PAIR), 1) < HEAD_DIM
+    same = jnp.where(row_head == col_head, 1.0, 0.0).astype(BF16)
+    first_head = lax.broadcasted_iota(jnp.int32, (HEAD_DIM, PAIR), 1) < HEAD_DIM
+
+    def numer_step(j):
+        parts = [vb[t, :, a:b] for t, a, b in cover(PAIR * j, PAIR * (j + 1), LANES)]
+        slab = jnp.concatenate(parts, axis=1)
+        zero = jnp.zeros_like(slab)
+        both = jnp.concatenate([jnp.where(first_head, slab, zero), jnp.where(first_head, zero, slab)], axis=0)
+        found = jnp.dot(qa[j, :, :PAIR], both, preferred_element_type=F32)
+        numer[j % 3, :, :PAIR] = found
+        sq[j % 3, :, :PAIR] = (found * found).astype(BF16)
+
+    far = pl.ds(pl.multiple_of((1 - space) * (tokens + width), width), width)
+    stores = []
+
+    def mixed_step(j):
+        total = jnp.dot(sq[j % 3, :, :PAIR], same, preferred_element_type=F32)
+        scale = lax.rsqrt(total * (1.0 / HEAD_DIM) + 1e-6)
+        normed = numer[j % 3, :, :PAIR] * scale
+        qa[j, :, :PAIR] = (ra[j, :, :PAIR].astype(F32) + normed * ga[j : j + 1, :PAIR]).astype(BF16)
+        t0, t1 = PAIR * j // LANES, PAIR * (j + 1) // LANES
+        if j == pairs - 1:
+            t1 = -(-dim // LANES)
+        for t in range(t0, t1):
+            lo, hi = LANES * t, min(dim, LANES * (t + 1))
+            parts = [qa[n, :, a:b] for n, a, b in cover(lo, hi, PAIR)]
+            value = jnp.concatenate(parts, axis=1) if len(parts) > 1 else parts[0]
+            mixed[width : width + tokens, lo:hi] = value[:tokens]
+            mixed[far, lo:hi] = value[tokens:]
+        lo, hi = LANES * t0, min(dim, LANES * t1)
+        store = pltpu.make_async_copy(mixed.at[:, lo:hi], o_hbm.at[:, lo:hi], out_sem.at[j])
+        store.start()
+        stores.append(store)
 
     for copy in loads:
         copy.wait()
-    for copy in edges:
-        copy.wait_recv()
-
-    def numer_step(m):
-        lo, w, heads, ks, ke = wins[m]
-        tile = 2 * m + other
-        to_other(ob, ob, tile, ag_s, ag_r, m).wait_recv()
-        to_other(vb, vb, tile, pv_s, pv_r, m).wait_recv()
-        phi = jnp.maximum(q[:, ks:ke], 0)
-        found = jnp.dot(phi, spread(vb, lo, w, heads, ks, ke), preferred_element_type=F32)
-        found = found + jnp.dot(phi, spread(ob, lo, w, heads, ks, ke), preferred_element_type=F32)
-        numer[:, lo : lo + w] = found
-        sq[:, lo : lo + w] = (found * found).astype(BF16)
-
-    far = pl.ds(pl.multiple_of((1 - space) * (tokens + width), width), width)
-    stores = []
-
-    def mixed_step(m):
-        lo, w, heads, ks, ke = wins[m]
-        from_head = (lax.broadcasted_iota(jnp.int32, (ke - ks, w), 0) + ks) // HEAD_DIM
-        to_head = (lax.broadcasted_iota(jnp.int32, (ke - ks, w), 1) + lo) // HEAD_DIM
-        same = jnp.where(from_head == to_head, 1.0, 0.0).astype(BF16)
-        total = jnp.dot(sq[:, ks:ke], same, preferred_element_type=F32)
-        scale = lax.rsqrt(total * (1.0 / HEAD_DIM) + 1e-6)
-        normed = numer[:, lo : lo + w] * scale
-        value = (res[:, lo : lo + w].astype(F32) + normed * gain_ref[lo : lo + w].reshape(1, w)).astype(BF16)
-        mixed[width : width + tokens, lo : lo + w] = value[:tokens]
-        mixed[far, lo : lo + w] = value[tokens:]
-        store = pltpu.make_async_copy(mixed.at[:, lo : lo + w], o_hbm.at[:, lo : lo + w], out_sem.at[m])
-        store.start()
-        stores.append(store)
-
-    last_in_chain(0, AHEAD)
-    for m in range(steps):
-        last_in_chain(m + AHEAD, m + AHEAD + 1)
-        numer_step(m)
-        if m > 0:
-            mixed_step(m - 1)
-    mixed_step(steps - 1)
+    realign(0, tokens)
+    for j in range(pairs):
+        ga[j : j + 1, :PAIR] = gain_ref[0:1, PAIR * j : PAIR * (j + 1)]
+
+    begun = 0
+    for j in range(steps + AHEAD):
+        if j < steps:
+            scan_step(j)
+        if j == AHEAD - 1:
+            for copy in edges:
+                copy.wait_recv()
+            realign(tokens, tokens + width)
+        m = j - AHEAD
+        if m < 0:
+            continue
+        to_other(vb, vb, 2 * m + other, pv_s, pv_r, m).wait_recv()
+        while begun < pairs and (PAIR * (begun + 1) - 1) // WINDOW <= m:
+            numer_step(begun)
+            if begun >= 2:
+                mixed_step(begun - 2)
+            begun += 1
+    mixed_step(pairs - 2)
+    mixed_step(pairs - 1)
 
     for copy in edges:
         copy.wait_send()
@@ -242,7 +251,6 @@
     def drain_step(j, _):
         mine, theirs = 2 * j + space, 2 * j + other
         to_other(pb, rb, theirs, rs_s, rs_r, j).wait_send()
-        to_other(ob, ob, mine, ag_s, ag_r, j).wait_send()
         to_frame(ob, yb, mine, y_s, y_r, j, twin).wait_send()
         to_other(vb, vb, mine, pv_s, pv_r, j).wait_send()
 
@@ -303,6 +311,7 @@
         sems = pltpu.SemaphoreType.DMA((steps,))
         two = pltpu.SemaphoreType.DMA((2,))
         ext = tokens + width
+        pairs = dim // PAIR
         mixed = pl.pallas_call(
             functools.partial(mix_kernel, frames, rows, width, dim),
             out_shape=jax.ShapeDtypeStruct((tokens + 2 * width, dim), BF16),
@@ -317,17 +326,21 @@
             ]
             + [pltpu.VMEM(state, BF16)] * 7
             + [
-                pltpu.VMEM((ext, dim), F32),
-                pltpu.VMEM((ext, dim), BF16),
+                pltpu.VMEM((pairs, ext, WINDOW), BF16),
+                pltpu.VMEM((pairs, ext, WINDOW), BF16),
+                pltpu.VMEM((pairs, WINDOW), F32),
+                pltpu.VMEM((3, ext, WINDOW), F32),
+                pltpu.VMEM((3, ext, WINDOW), BF16),
                 pltpu.VMEM((tokens + 2 * width, dim), BF16),
                 pltpu.SemaphoreType.DMA((2, -(-dim // PIECE))),
                 two,
                 two,
                 two,
             ]
-            + [sems] * 11,
+            + [sems] * 8
+            + [pltpu.SemaphoreType.DMA((pairs,))],
             compiler_params=pltpu.CompilerParams(collective_id=0, has_side_effects=True, vmem_limit_bytes=56 << 20),
-        )(flat(queries), flat(keys), flat(values), flat(residual), attn_gain, )
+        )(flat(queries), flat(keys), flat(values), flat(residual), attn_gain.reshape(1, dim))
         out = pl.pallas_call(
             functools.partial(conv_kernel, rows, width),
             out_shape=jax.ShapeDtypeStruct((tokens, dim), BF16),

time: 35.7 us -> 35.4 us (level)
  Pallas kernels: 35.1 us -> 33.7 us
  local copies, waits for them, and re-layouts: 0 us -> 1.31 us
    pallas_call x1, Pallas kernels: 26.4 us -> 25.1 us  [on_device(): pl.pallas_call(functools.partial(mix_kernel, frames, rows, width, dim), o...]
    reshape x0 -> x1, local copies, waits for them, and re-layouts: none -> 1.31 us  [on_device(): attn_gain.reshape(1, dim)]
where the time goes in v1:
time: 35.4 us; the launch traced here: 35.1 us
  Pallas kernels  33.7 us (95%)
  local copies, waits for them, and re-layouts  1.31 us (4%)
    pallas_call x1, Pallas kernels, on_device(): pl.pallas_call(functools.partial(mix_kernel, frames, rows, width, dim), o...  25.1 us
    pallas_call x1, Pallas kernels, on_device(): pl.pallas_call(functools.partial(conv_kernel, rows, width), out_shape=jax...  8.69 us
    reshape x1, local copies, waits for them, and re-layouts, on_device(): attn_gain.reshape(1, dim)  1.31 us

profile of v1, /device:TPU:27, one launch (start us, length us, event | category | flops | bytes accessed | tf_op | source)
XLA Modules:
  0.0 35.1 jit_solution(2770129029250597951)
XLA Ops:
  0.0 1.3 %reshape.22.gain_ref = f32[1,2240]{1,0:T(1,128)} reshape(f32[2240]{0:T(1024)} %param.11) | data formatting | bytes 17920 | tf_op jit(solution)/shard_map/reshape | solution.py:343
  1.3 25.1 %shard_map.73.m_ref = bf16[640,2240]{1,0:T(8,128)(2,1)} custom-call(bf16[480,2240]{1,0:T(8,128)(2,1)} %bitcast.5, bf16[480,2240]{1,0:T(8,128)(2,1)} %bitcast.6, bf16[480,2240]{1,0:T(8,128)(2,1)} %bitcast.7, bf16[480,2240]{1,0:T(8,128)(2,1)} %bitcast.8, f32[1,2240]{1,0:T(1,128)} %reshape.22.gain_ref), custom_call_target="tpu_custom_call" | custom-call | tf_op jit(solution)/shard_map/pallas_call | solution.py:315
  26.4 8.7 %shard_map.74 = bf16[480,2240]{1,0:T(8,128)(2,1)} custom-call(bf16[640,2240]{1,0:T(8,128)(2,1)} %shard_map.73.m_ref, f32[9,2240]{1,0:T(8,128)} %vt_ref.1, f32[9,2240]{1,0:T(8,128)} %gt_ref.1), custom_call_target="tpu_custom_call" | custom-call | tf_op jit(solution)/shard_map/pallas_call | solution.py:344

commit v2 on v1

--- a/solution.py
+++ b/solution.py
@@ -14,7 +14,10 @@
 PIECE = 384
 BLOCK = 384
 PAIR = 2 * HEAD_DIM
-LAG = 4
+LAG = 3
+LEAD = 2
+GROUP = 2
+FETCH = 3
 AHEAD = 2
 F32, BF16 = jnp.float32, jnp.bfloat16
 
@@ -24,16 +27,14 @@
     for lo in range(0, dim, WINDOW):
         w = min(WINDOW, dim - lo)
         h0, h1 = lo // HEAD_DIM, (lo + w - 1) // HEAD_DIM
-        ks = HEAD_DIM * h0 // LANES * LANES
-        ke = min(dim, -(-HEAD_DIM * (h1 + 1) // LANES) * LANES)
-        out.append((lo, w, range(h0, h1 + 1), ks, ke))
+        out.append((lo, w, range(h0, h1 + 1)))
     return out
 
 
 def mix_kernel(
     frames, rows, width, dim,
     q_hbm, k_hbm, v_hbm, r_hbm, gain_ref, o_hbm,
-    q, k, v, res, st, pb, rb, ob, yb, pr, ps, vb, qa, ra, ga, numer, sq, mixed,
+    q, k, v, kt, res, st, pb, rb, ob, yb, pr, ps, vb, qa, ra, ga, numer, sq, mixed,
     kv_sem, load_sem, edge_s, edge_r, rs_s, rs_r, y_s, y_r, z_s, z_r, pv_s, pv_r, out_sem,
 ):
     tokens = rows * width
@@ -79,8 +80,6 @@
     st[tiles - 1] = jnp.zeros(st.shape[1:], F32)
     mixed[pl.ds(pl.multiple_of(space * (tokens + width), width), width), :] = jnp.zeros((width, dim), BF16)
 
-    pl.semaphore_wait(barrier, 2 + jnp.where(has_prev, 1, 0) + jnp.where(has_next, 1, 0))
-
     def to_other(src, dst, tile, send, recv, j):
         return pltpu.make_async_remote_copy(
             src_ref=src.at[tile], dst_ref=dst.at[tile], send_sem=send.at[j], recv_sem=recv.at[j],
@@ -113,30 +112,36 @@
         ob[tile] = total.astype(BF16)
         to_frame(ob, yb, tile, y_s, y_r, j, twin).start()
 
-    ready = 0
+    ready, turned = 0, 0
     for m in range(steps):
-        lo, w, heads, ks, ke = wins[m]
-        while cuts[ready] < ke:
+        lo, w, heads = wins[m]
+        k0, k1 = HEAD_DIM * heads[0], HEAD_DIM * (heads[-1] + 1)
+        while cuts[ready] < max(k1, lo + w):
             for copy in kv_loads[ready]:
                 copy.wait()
             ready += 1
-            if ready == len(kv_loads):
-                for copy in loads:
-                    copy.start()
-        full = lax.dot_general(
-            jnp.maximum(k[:, ks:ke], 0), v[:, lo : lo + w], (((0,), (0,)), ((), ())), preferred_element_type=F32
-        )
+        if m == FETCH:
+            for copy in loads:
+                copy.start()
+        while turned < k1:
+            top = min(dim, turned + LANES)
+            kt[turned:top, :] = jnp.maximum(k[:, turned:top], 0).T
+            turned = top
+        full = jnp.dot(kt[k0:k1, :], v[:, lo : lo + w], preferred_element_type=F32)
         owner = head_of(lo, w)
-        slab = jnp.zeros((HEAD_DIM, w), F32)
-        for h in heads:
-            at = HEAD_DIM * h - ks
+        slab = full[:HEAD_DIM]
+        for h in heads[1:]:
+            at = HEAD_DIM * h - k0
             slab = jnp.where(owner == h, full[at : at + HEAD_DIM, :], slab)
         for part in range(-(-w // LANES)):
             tile = lo // LANES + part
             wide = min(LANES, w - part * LANES)
             st[tile, :, :wide] = slab[:, part * LANES : part * LANES + wide]
             pb[tile] = st[tile].astype(BF16)
-        to_other(pb, rb, 2 * m + other, rs_s, rs_r, m).start()
+        if m == LEAD - 1:
+            pl.semaphore_wait(barrier, 2 + jnp.where(has_prev, 1, 0) + jnp.where(has_next, 1, 0))
+        for n in range(m + 1) if m == LEAD - 1 else range(m, m + 1) if m >= LEAD else ():
+            to_other(pb, rb, 2 * n + other, rs_s, rs_r, n).start()
         if m >= LAG:
             own_step(m - LAG)
     for m in range(max(0, steps - LAG), steps):
@@ -169,8 +174,8 @@
 
     pairs = dim // PAIR
 
-    def realign(r0, r1):
-        for j in range(pairs):
+    def realign(r0, r1, j0, j1):
+        for j in range(j0, min(j1, pairs)):
             qa[j, r0:r1, :PAIR] = jnp.maximum(q[r0:r1, PAIR * j : PAIR * (j + 1)], 0)
             ra[j, r0:r1, :PAIR] = res[r0:r1, PAIR * j : PAIR * (j + 1)]
 
@@ -194,16 +199,16 @@
         zero = jnp.zeros_like(slab)
         both = jnp.concatenate([jnp.where(first_head, slab, zero), jnp.where(first_head, zero, slab)], axis=0)
         found = jnp.dot(qa[j, :, :PAIR], both, preferred_element_type=F32)
-        numer[j % 3, :, :PAIR] = found
-        sq[j % 3, :, :PAIR] = (found * found).astype(BF16)
+        numer[j % (2 * GROUP), :, :PAIR] = found
+        sq[j % (2 * GROUP), :, :PAIR] = (found * found).astype(BF16)
 
     far = pl.ds(pl.multiple_of((1 - space) * (tokens + width), width), width)
     stores = []
 
     def mixed_step(j):
-        total = jnp.dot(sq[j % 3, :, :PAIR], same, preferred_element_type=F32)
+        total = jnp.dot(sq[j % (2 * GROUP), :, :PAIR], same, preferred_element_type=F32)
         scale = lax.rsqrt(total * (1.0 / HEAD_DIM) + 1e-6)
-        normed = numer[j % 3, :, :PAIR] * scale
+        normed = numer[j % (2 * GROUP), :, :PAIR] * scale
         qa[j, :, :PAIR] = (ra[j, :, :PAIR].astype(F32) + normed * ga[j : j + 1, :PAIR]).astype(BF16)
         t0, t1 = PAIR * j // LANES, PAIR * (j + 1) // LANES
         if j == pairs - 1:
@@ -219,31 +224,49 @@
         store.start()
         stores.append(store)
 
-    for copy in loads:
-        copy.wait()
-    realign(0, tokens)
     for j in range(pairs):
-        ga[j : j + 1, :PAIR] = gain_ref[0:1, PAIR * j : PAIR * (j + 1)]
+        ga[j : j + 1, :PAIR] = gain_ref[PAIR * j : PAIR * (j + 1)].reshape(1, PAIR)
+
+    def prepare(stage):
+        if stage == 0:
+            for copy in loads:
+                copy.wait()
+        if stage == 1:
+            for copy in edges:
+                copy.wait_recv()
+            realign(tokens, tokens + width, 0, pairs)
+        realign(0, tokens, 3 * stage, 3 * stage + 3)
+
+    stages = -(-pairs // 3)
+
+    @pl.when(has_prev)
+    def _():
+        for stage in range(stages):
+            prepare(stage)
 
     begun = 0
     for j in range(steps + AHEAD):
         if j < steps:
             scan_step(j)
-        if j == AHEAD - 1:
-            for copy in edges:
-                copy.wait_recv()
-            realign(tokens, tokens + width)
+        if j < stages:
+            @pl.when(jnp.logical_not(has_prev))
+            def _():
+                prepare(j)
         m = j - AHEAD
         if m < 0:
             continue
         to_other(vb, vb, 2 * m + other, pv_s, pv_r, m).wait_recv()
-        while begun < pairs and (PAIR * (begun + 1) - 1) // WINDOW <= m:
-            numer_step(begun)
-            if begun >= 2:
-                mixed_step(begun - 2)
-            begun += 1
-    mixed_step(pairs - 2)
-    mixed_step(pairs - 1)
+        while begun < pairs:
+            until = min(pairs, begun + GROUP)
+            if (PAIR * until - 1) // WINDOW > m:
+                break
+            for n in range(begun, until):
+                numer_step(n)
+            for n in range(max(0, begun - GROUP), begun):
+                mixed_step(n)
+            begun = until
+    for n in range(max(0, pairs - GROUP) if pairs % GROUP == 0 else pairs - pairs % GROUP, pairs):
+        mixed_step(n)
 
     for copy in edges:
         copy.wait_send()
@@ -321,6 +344,7 @@
                 pltpu.VMEM((ext, dim), BF16),
                 pltpu.VMEM((tokens, dim), BF16),
                 pltpu.VMEM((tokens, dim), BF16),
+                pltpu.VMEM((dim, tokens), BF16),
                 pltpu.VMEM((ext, dim), BF16),
                 pltpu.VMEM(state, F32),
             ]
@@ -329,8 +353,8 @@
                 pltpu.VMEM((pairs, ext, WINDOW), BF16),
                 pltpu.VMEM((pairs, ext, WINDOW), BF16),
                 pltpu.VMEM((pairs, WINDOW), F32),
-                pltpu.VMEM((3, ext, WINDOW), F32),
-                pltpu.VMEM((3, ext, WINDOW), BF16),
+                pltpu.VMEM((2 * GROUP, ext, WINDOW), F32),
+                pltpu.VMEM((2 * GROUP, ext, WINDOW), BF16),
                 pltpu.VMEM((tokens + 2 * width, dim), BF16),
                 pltpu.SemaphoreType.DMA((2, -(-dim // PIECE))),
                 two,
@@ -340,7 +364,7 @@
             + [sems] * 8
             + [pltpu.SemaphoreType.DMA((pairs,))],
             compiler_params=pltpu.CompilerParams(collective_id=0, has_side_effects=True, vmem_limit_bytes=56 << 20),
-        )(flat(queries), flat(keys), flat(values), flat(residual), attn_gain.reshape(1, dim))
+        )(flat(queries), flat(keys), flat(values), flat(residual), attn_gain)
         out = pl.pallas_call(
             functools.partial(conv_kernel, rows, width),
             out_shape=jax.ShapeDtypeStruct((tokens, dim), BF16),

time: 35.4 us -> 33.8 us (0.955)
  local copies, waits for them, and re-layouts: 1.31 us -> 0 us
    reshape x1 -> x0, local copies, waits for them, and re-layouts: 1.31 us -> none  [on_device(): attn_gain.reshape(1, dim)]
where the time goes in v2:
time: 33.8 us; the launch traced here: 33.5 us
  Pallas kernels  33.5 us (99%)
    pallas_call x1, Pallas kernels, on_device(): pl.pallas_call(functools.partial(mix_kernel, frames, rows, width, dim), o...  24.8 us
    pallas_call x1, Pallas kernels, on_device(): pl.pallas_call(functools.partial(conv_kernel, rows, width), out_shape=jax...  8.69 us

profile of v2, /device:TPU:27, one launch (start us, length us, event | category | flops | bytes accessed | tf_op | source)
XLA Modules:
  0.0 33.5 jit_solution(10525743886760238413)
XLA Ops:
  0.0 24.8 %shard_map.73.m_ref = bf16[640,2240]{1,0:T(8,128)(2,1)} custom-call(bf16[480,2240]{1,0:T(8,128)(2,1)} %bitcast.5, bf16[480,2240]{1,0:T(8,128)(2,1)} %bitcast.6, bf16[480,2240]{1,0:T(8,128)(2,1)} %bitcast.7, bf16[480,2240]{1,0:T(8,128)(2,1)} %bitcast.8, f32[2240]{0:T(1024)} %gain_ref.1), custom_call_target="tpu_custom_call" | custom-call | tf_op jit(solution)/shard_map/pallas_call | solution.py:338
  24.8 8.7 %shard_map.74 = bf16[480,2240]{1,0:T(8,128)(2,1)} custom-call(bf16[640,2240]{1,0:T(8,128)(2,1)} %shard_map.73.m_ref, f32[9,2240]{1,0:T(8,128)} %vt_ref.1, f32[9,2240]{1,0:T(8,128)} %gt_ref.1), custom_call_target="tpu_custom_call" | custom-call | tf_op jit(solution)/shard_map/pallas_call | solution.py:368

commit v3 on v2

--- a/solution.py
+++ b/solution.py
@@ -12,12 +12,10 @@
 WINDOW = 256
 PAD = 8
 PIECE = 384
-BLOCK = 384
 PAIR = 2 * HEAD_DIM
 LAG = 3
 LEAD = 2
 GROUP = 2
-FETCH = 3
 AHEAD = 2
 F32, BF16 = jnp.float32, jnp.bfloat16
 
@@ -33,9 +31,9 @@
 
 def mix_kernel(
     frames, rows, width, dim,
-    q_hbm, k_hbm, v_hbm, r_hbm, gain_ref, o_hbm,
-    q, k, v, kt, res, st, pb, rb, ob, yb, pr, ps, vb, qa, ra, ga, numer, sq, mixed,
-    kv_sem, load_sem, edge_s, edge_r, rs_s, rs_r, y_s, y_r, z_s, z_r, pv_s, pv_r, out_sem,
+    q_hbm, k_hbm, v_hbm, r_hbm, gain_hbm, vt_hbm, gt_hbm, o_ref,
+    q, k, v, kt, res, st, pb, rb, ob, yb, pr, ps, vb, qa, ra, gain_ref, ga, vt_ref, gt_ref, taps, numer, sq, mixed, x32,
+    kv_sem, load_sem, edge_s, edge_r, rs_s, rs_r, y_s, y_r, z_s, z_r, pv_s, pv_r, small_sem,
 ):
     tokens = rows * width
     tiles = st.shape[0]
@@ -59,12 +57,23 @@
             ]
         )
     loads = [
-        pltpu.make_async_copy(src, dst.at[0:tokens], load_sem.at[i]) for i, (src, dst) in enumerate(((q_hbm, q), (r_hbm, res)))
+        [
+            pltpu.make_async_copy(src.at[:, lo:hi], dst.at[0:tokens, lo:hi], load_sem.at[c, i])
+            for c, (src, dst) in enumerate(((q_hbm, q), (r_hbm, res)))
+        ]
+        for i, (lo, hi) in enumerate(zip(cuts, cuts[1:]))
     ]
     for copies in kv_loads:
         for copy in copies:
             copy.start()
 
+    small = [
+        pltpu.make_async_copy(src, dst, small_sem.at[i])
+        for i, (src, dst) in enumerate(((gain_hbm, gain_ref), (vt_hbm, vt_ref), (gt_hbm, gt_ref)))
+    ]
+    for copy in small:
+        copy.start()
+
     barrier = pltpu.get_barrier_semaphore()
     pl.semaphore_signal(barrier, inc=1, device_id={"space": other})
     pl.semaphore_signal(barrier, inc=1, device_id={"frame": twin})
@@ -78,7 +87,9 @@
         pl.semaphore_signal(barrier, inc=1, device_id={"frame": frame + 2})
 
     st[tiles - 1] = jnp.zeros(st.shape[1:], F32)
-    mixed[pl.ds(pl.multiple_of(space * (tokens + width), width), width), :] = jnp.zeros((width, dim), BF16)
+    x32[...] = jnp.zeros(x32.shape, F32)
+    taps[...] = jnp.zeros(taps.shape, F32)
+    mixed[:, dim:] = jnp.zeros((mixed.shape[0], mixed.shape[1] - dim), BF16)
 
     def to_other(src, dst, tile, send, recv, j):
         return pltpu.make_async_remote_copy(
@@ -93,12 +104,15 @@
         )
 
     edges = [
-        pltpu.make_async_remote_copy(
-            src_ref=src.at[pl.ds(pl.multiple_of(other * (tokens - width), width), width)],
-            dst_ref=dst.at[tokens : tokens + width],
-            send_sem=edge_s.at[i], recv_sem=edge_r.at[i], device_id={"space": other},
-        )
-        for i, (src, dst) in enumerate(((q_hbm, q), (r_hbm, res)))
+        [
+            pltpu.make_async_remote_copy(
+                src_ref=src.at[pl.ds(pl.multiple_of(other * (tokens - width), width), width), lo:hi],
+                dst_ref=dst.at[tokens : tokens + width, lo:hi],
+                send_sem=edge_s.at[c, i], recv_sem=edge_r.at[c, i], device_id={"space": other},
+            )
+            for c, (src, dst) in enumerate(((q_hbm, q), (r_hbm, res)))
+        ]
+        for i, (lo, hi) in enumerate(zip(cuts, cuts[1:]))
     ]
 
     def head_of(lo, w):
@@ -112,7 +126,7 @@
         ob[tile] = total.astype(BF16)
         to_frame(ob, yb, tile, y_s, y_r, j, twin).start()
 
-    ready, turned = 0, 0
+    ready, turned, fetched = 0, 0, 0
     for m in range(steps):
         lo, w, heads = wins[m]
         k0, k1 = HEAD_DIM * heads[0], HEAD_DIM * (heads[-1] + 1)
@@ -120,9 +134,6 @@
             for copy in kv_loads[ready]:
                 copy.wait()
             ready += 1
-        if m == FETCH:
-            for copy in loads:
-                copy.start()
         while turned < k1:
             top = min(dim, turned + LANES)
             kt[turned:top, :] = jnp.maximum(k[:, turned:top], 0).T
@@ -144,10 +155,16 @@
             to_other(pb, rb, 2 * n + other, rs_s, rs_r, n).start()
         if m >= LAG:
             own_step(m - LAG)
+        if m >= LEAD:
+            for copies in loads[fetched : fetched + 1] + edges[fetched : fetched + 1]:
+                for copy in copies:
+                    copy.start()
+            fetched += 1
+    for copies in loads[fetched:] + edges[fetched:]:
+        for copy in copies:
+            copy.start()
     for m in range(max(0, steps - LAG), steps):
         own_step(m)
-    for copy in edges:
-        copy.start()
 
     def scan_step(j):
         tile = 2 * j + space
@@ -202,38 +219,75 @@
         numer[j % (2 * GROUP), :, :PAIR] = found
         sq[j % (2 * GROUP), :, :PAIR] = (found * found).astype(BF16)
 
-    far = pl.ds(pl.multiple_of((1 - space) * (tokens + width), width), width)
-    stores = []
-
     def mixed_step(j):
         total = jnp.dot(sq[j % (2 * GROUP), :, :PAIR], same, preferred_element_type=F32)
         scale = lax.rsqrt(total * (1.0 / HEAD_DIM) + 1e-6)
         normed = numer[j % (2 * GROUP), :, :PAIR] * scale
         qa[j, :, :PAIR] = (ra[j, :, :PAIR].astype(F32) + normed * ga[j : j + 1, :PAIR]).astype(BF16)
-        t0, t1 = PAIR * j // LANES, PAIR * (j + 1) // LANES
-        if j == pairs - 1:
-            t1 = -(-dim // LANES)
-        for t in range(t0, t1):
+        for t in range(PAIR * j // LANES, done(j + 1)):
             lo, hi = LANES * t, min(dim, LANES * (t + 1))
             parts = [qa[n, :, a:b] for n, a, b in cover(lo, hi, PAIR)]
-            value = jnp.concatenate(parts, axis=1) if len(parts) > 1 else parts[0]
-            mixed[width : width + tokens, lo:hi] = value[:tokens]
-            mixed[far, lo:hi] = value[tokens:]
-        lo, hi = LANES * t0, min(dim, LANES * t1)
-        store = pltpu.make_async_copy(mixed.at[:, lo:hi], o_hbm.at[:, lo:hi], out_sem.at[j])
-        store.start()
-        stores.append(store)
-
+            mixed[:, lo:hi] = jnp.concatenate(parts, axis=1) if len(parts) > 1 else parts[0]
+
+    def done(j):
+        return -(-dim // LANES) if j == pairs else PAIR * j // LANES
+
+    pitch = width + 2 * PAD
+    far = pl.multiple_of((1 - space) * (rows + 1) * pitch + PAD, PAD)
+    chunk = 16
+
+    def conv_tile(at, keep):
+        for row in range(rows):
+            first = (row + 1) * pitch + PAD
+            x32[first : first + width, :] = mixed[row * width : (row + 1) * width, at].astype(F32)
+        x32[pl.ds(far, width), :] = mixed[tokens:, at].astype(F32)
+        tv = [jnp.broadcast_to(taps[0, n : n + 1, at], (chunk, LANES)) for n in range(9)]
+        tg = [jnp.broadcast_to(taps[1, n : n + 1, at], (chunk, LANES)) for n in range(9)]
+        for row in range(rows):
+            for off in range(0, width, chunk):
+                cv, cg = None, None
+                for n in range(9):
+                    start = (row + n // 3) * pitch + PAD - 1 + n % 3 + off
+                    x = x32[start : start + chunk, :]
+                    cv = tv[n] * x if cv is None else cv + tv[n] * x
+                    cg = tg[n] * x if cg is None else cg + tg[n] * x
+                centre = (row + 1) * pitch + PAD + off
+                half = 0.5 * cg
+                value = (x32[centre : centre + chunk, :] + cv * (half + half * jnp.tanh(half))).astype(BF16)
+                first = row * width + off
+                if keep == LANES:
+                    o_ref[first : first + chunk, at] = value
+                else:
+                    o_ref[first : first + chunk, dim - keep : dim] = value[:, :keep]
+
+    def conv_step(t0, t1):
+        whole = min(t1, dim // LANES)
+
+        def one(t, _):
+            conv_tile(pl.ds(pl.multiple_of(t * LANES, LANES), LANES), LANES)
+            return 0
+
+        if whole > t0:
+            lax.fori_loop(t0, whole, one, 0)
+        if t1 > whole:
+            conv_tile(slice(whole * LANES, t1 * LANES), dim - whole * LANES)
+
+    for copy in small:
+        copy.wait()
+    taps[0, 0:9, 0:dim] = vt_ref[...]
+    taps[1, 0:9, 0:dim] = gt_ref[...]
     for j in range(pairs):
         ga[j : j + 1, :PAIR] = gain_ref[PAIR * j : PAIR * (j + 1)].reshape(1, PAIR)
 
     def prepare(stage):
         if stage == 0:
-            for copy in loads:
-                copy.wait()
-        if stage == 1:
-            for copy in edges:
-                copy.wait_recv()
+            for copies in loads:
+                for copy in copies:
+                    copy.wait()
+        if stage == stages - 1:
+            for copies in edges:
+                for copy in copies:
+                    copy.wait_recv()
             realign(tokens, tokens + width, 0, pairs)
         realign(0, tokens, 3 * stage, 3 * stage + 3)
 
@@ -264,12 +318,17 @@
                 numer_step(n)
             for n in range(max(0, begun - GROUP), begun):
                 mixed_step(n)
+            if begun:
+                conv_step(done(max(0, begun - GROUP)), done(begun))
             begun = until
-    for n in range(max(0, pairs - GROUP) if pairs % GROUP == 0 else pairs - pairs % GROUP, pairs):
+    last = (pairs - 1) // GROUP * GROUP
+    for n in range(last, pairs):
         mixed_step(n)
-
-    for copy in edges:
-        copy.wait_send()
+    conv_step(done(last), done(pairs))
+
+    for copies in edges:
+        for copy in copies:
+            copy.wait_send()
 
     def drain_step(j, _):
         mine, theirs = 2 * j + space, 2 * j + other
@@ -284,41 +343,6 @@
         return 0
 
     lax.fori_loop(0, steps, drain_step, 0)
-    for store in stores:
-        store.wait()
-
-
-def conv_kernel(rows, width, m_ref, vt_ref, gt_ref, o_ref, x32):
-    step = width + 2 * PAD
-    part = 16
-
-    @pl.when(pl.program_id(0) == 0)
-    def _():
-        x32[...] = jnp.zeros_like(x32)
-
-    def tile_step(t, _):
-        at = pl.ds(pl.multiple_of(t * LANES, LANES), LANES)
-        for row in range(rows + 2):
-            x32[row * step + PAD : row * step + PAD + width, :] = m_ref[row * width : (row + 1) * width, at].astype(F32)
-        taps = [
-            (jnp.broadcast_to(vt_ref[n : n + 1, at], (part, LANES)), jnp.broadcast_to(gt_ref[n : n + 1, at], (part, LANES)))
-            for n in range(9)
-        ]
-        for row in range(rows):
-            for off in range(0, width, part):
-                cv, cg = None, None
-                for n in range(9):
-                    start = (row + n // 3) * step + PAD - 1 + n % 3 + off
-                    x = x32[start : start + part, :]
-                    cv = taps[n][0] * x if cv is None else cv + taps[n][0] * x
-                    cg = taps[n][1] * x if cg is None else cg + taps[n][1] * x
-                centre = (row + 1) * step + PAD + off
-                half = 0.5 * cg
-                value = x32[centre : centre + part, :] + cv * (half + half * jnp.tanh(half))
-                o_ref[row * width + off : row * width + off + part, at] = value.astype(BF16)
-        return 0
-
-    lax.fori_loop(0, o_ref.shape[1] // LANES, tile_step, 0)
 
 
 def solution(mesh):
@@ -332,14 +356,16 @@
         anywhere = pl.BlockSpec(memory_space=pl.ANY)
         state = (2 * steps, HEAD_DIM, LANES)
         sems = pltpu.SemaphoreType.DMA((steps,))
-        two = pltpu.SemaphoreType.DMA((2,))
+        pieces = pltpu.SemaphoreType.DMA((2, -(-dim // PIECE)))
         ext = tokens + width
         pairs = dim // PAIR
-        mixed = pl.pallas_call(
+        across = -(-dim // LANES) * LANES
+        operands = (flat(queries), flat(keys), flat(values), flat(residual), attn_gain, value_taps, gate_taps)
+        out = pl.pallas_call(
             functools.partial(mix_kernel, frames, rows, width, dim),
-            out_shape=jax.ShapeDtypeStruct((tokens + 2 * width, dim), BF16),
-            in_specs=[anywhere] * 4 + [pl.BlockSpec(memory_space=pltpu.VMEM)],
-            out_specs=anywhere,
+            out_shape=jax.ShapeDtypeStruct((tokens, dim), BF16),
+            in_specs=[anywhere] * 7,
+            out_specs=pl.BlockSpec(memory_space=pltpu.VMEM),
             scratch_shapes=[
                 pltpu.VMEM((ext, dim), BF16),
                 pltpu.VMEM((tokens, dim), BF16),
@@ -352,31 +378,24 @@
             + [
                 pltpu.VMEM((pairs, ext, WINDOW), BF16),
                 pltpu.VMEM((pairs, ext, WINDOW), BF16),
+                pltpu.VMEM((dim,), F32),
                 pltpu.VMEM((pairs, WINDOW), F32),
+                pltpu.VMEM((9, dim), F32),
+                pltpu.VMEM((9, dim), F32),
+                pltpu.VMEM((2, 16, across), F32),
                 pltpu.VMEM((2 * GROUP, ext, WINDOW), F32),
                 pltpu.VMEM((2 * GROUP, ext, WINDOW), BF16),
-                pltpu.VMEM((tokens + 2 * width, dim), BF16),
-                pltpu.SemaphoreType.DMA((2, -(-dim // PIECE))),
-                two,
-                two,
-                two,
+                pltpu.VMEM((ext, across), BF16),
+                pltpu.VMEM(((rows + 2) * (width + 2 * PAD), LANES), F32),
+                pieces,
+                pieces,
+                pieces,
+                pieces,
             ]
             + [sems] * 8
-            + [pltpu.SemaphoreType.DMA((pairs,))],
-            compiler_params=pltpu.CompilerParams(collective_id=0, has_side_effects=True, vmem_limit_bytes=56 << 20),
-        )(flat(queries), flat(keys), flat(values), flat(residual), attn_gain)
-        out = pl.pallas_call(
-            functools.partial(conv_kernel, rows, width),
-            out_shape=jax.ShapeDtypeStruct((tokens, dim), BF16),
-            grid=(-(-dim // BLOCK),),
-            in_specs=[
-                pl.BlockSpec((tokens + 2 * width, BLOCK), lambda c: (0, c)),
-                pl.BlockSpec((9, BLOCK), lambda c: (0, c)),
-                pl.BlockSpec((9, BLOCK), lambda c: (0, c)),
-            ],
-            out_specs=pl.BlockSpec((tokens, BLOCK), lambda c: (0, c)),
-            scratch_shapes=[pltpu.VMEM(((rows + 2) * (width + 2 * PAD), LANES), F32)],
-        )(mixed, value_taps, gate_taps)
+            + [pltpu.SemaphoreType.DMA((3,))],
+            compiler_params=pltpu.CompilerParams(collective_id=0, has_side_effects=True, vmem_limit_bytes=50 << 20),
+        )(*(pltpu.with_memory_space_constraint(a, pltpu.HBM) for a in operands))
         return out.reshape(1, rows, width, dim)
 
     placed = P(("groups", "frame"), "space", None, None)

time: 33.8 us -> 30.5 us (0.902)
  Pallas kernels: 33.5 us -> 29 us
  local copies, waits for them, and re-layouts: 0 us -> 1.36 us
    pallas_call x1 -> x0, Pallas kernels: 8.69 us -> none  [on_device(): pl.pallas_call(functools.partial(conv_kernel, rows, width), out_shape=jax...]
    pallas_call x1, Pallas kernels: 24.8 us -> 29 us  [on_device(): pl.pallas_call(functools.partial(mix_kernel, frames, rows, width, dim), o...]
    unnamed x0 -> x1, local copies, waits for them, and re-layouts: none -> 1.36 us
where the time goes in v3:
time: 30.5 us; the launch traced here: 30.4 us
  Pallas kernels  29 us (95%)
  local copies, waits for them, and re-layouts  1.36 us (4%)
    pallas_call x1, Pallas kernels, on_device(): pl.pallas_call(functools.partial(mix_kernel, frames, rows, width, dim), o...  29 us
    unnamed x1, local copies, waits for them, and re-layouts  1.36 us

profile of v3, /device:TPU:27, one launch (start us, length us, event | category | flops | bytes accessed | tf_op | source)
XLA Modules:
  0.0 30.4 jit_solution(791280513911800799)
XLA Ops:
  0.0 29.0 %shard_map.73 = bf16[480,2240]{1,0:T(8,128)(2,1)S(1)} custom-call(bf16[480,2240]{1,0:T(8,128)(2,1)} %bitcast.6, bf16[480,2240]{1,0:T(8,128)(2,1)} %bitcast.7, bf16[480,2240]{1,0:T(8,128)(2,1)} %bitcast.8, bf16[480,2240]{1,0:T(8,128)(2,1)} %bitcast.9, f32[2240]{0:T(1024)} %gain_hbm.1, f32[9,2240]{1,0:T(8,128)} %vt_hbm.1, f32[9,2240]{1,0:T(8,128)} %gt_hbm.1), custom_call_target="tpu_custom_call" | custom-call | tf_op jit(solution)/shard_map/pallas_call | solution.py:364
  29.0 1.4 %copy.9 = bf16[1,6,80,2240]{3,2,1,0:T(8,128)(2,1)} copy(bf16[1,6,80,2240]{3,2,1,0:T(8,128)(2,1)S(1)} %bitcast.5) | data formatting | bytes 4300800

commit v4 on v3

--- a/solution.py
+++ b/solution.py
@@ -13,10 +13,12 @@
 PAD = 8
 PIECE = 384
 PAIR = 2 * HEAD_DIM
-LAG = 3
-LEAD = 2
+LAG = 2
+LEAD = 1
+EARLY = 7
+SHARE = 4
 GROUP = 2
-AHEAD = 2
+FIRST, MIDDLE, LAST = 6, 4, 2
 F32, BF16 = jnp.float32, jnp.bfloat16
 
 
@@ -97,9 +99,13 @@
             device_id={"space": other},
         )
 
-    def to_frame(src, dst, tile, send, recv, j, target):
+    cut = HEAD_DIM // 32 * 16
+    halves = ((0, cut), (cut, HEAD_DIM))
+
+    def to_frame(src, dst, tile, send, recv, j, half, target):
+        r0, r1 = halves[half]
         return pltpu.make_async_remote_copy(
-            src_ref=src.at[tile], dst_ref=dst.at[tile], send_sem=send.at[j], recv_sem=recv.at[j],
+            src_ref=src.at[tile, r0:r1], dst_ref=dst.at[tile, r0:r1], send_sem=send.at[half, j], recv_sem=recv.at[half, j],
             device_id={"frame": target},
         )
 
@@ -124,7 +130,28 @@
         total = st[tile] + rb[tile].astype(F32)
         st[tile] = total
         ob[tile] = total.astype(BF16)
-        to_frame(ob, yb, tile, y_s, y_r, j, twin).start()
+        for half in range(2):
+            to_frame(ob, yb, tile, y_s, y_r, j, half, twin).start()
+
+    def scan_step(j, lead):
+        tile = 2 * j + space
+        for half, (r0, r1) in enumerate(halves):
+            to_frame(ob, yb, tile, y_s, y_r, j, half, twin).wait_recv()
+            beside = yb[tile, r0:r1].astype(F32)
+            mine = st[tile, r0:r1]
+            if lead:
+                before = jnp.zeros_like(mine)
+            else:
+                to_frame(ps, pr, tile, z_s, z_r, j, half, frame - 2).wait_recv()
+                before = pr[tile, r0:r1].astype(F32)
+
+            @pl.when(has_next)
+            def _():
+                ps[tile, r0:r1] = (before + (mine + beside)).astype(BF16)
+                to_frame(ps, pr, tile, z_s, z_r, j, half, frame + 2).start()
+
+            vb[tile, r0:r1] = (before + beside * odd.astype(F32) + mine).astype(BF16)
+        to_other(vb, vb, tile, pv_s, pv_r, j).start()
 
     ready, turned, fetched = 0, 0, 0
     for m in range(steps):
@@ -160,34 +187,15 @@
                 for copy in copies:
                     copy.start()
             fetched += 1
+        if m >= EARLY:
+            @pl.when(jnp.logical_not(has_prev))
+            def _():
+                scan_step(m - EARLY, True)
     for copies in loads[fetched:] + edges[fetched:]:
         for copy in copies:
             copy.start()
     for m in range(max(0, steps - LAG), steps):
         own_step(m)
-
-    def scan_step(j):
-        tile = 2 * j + space
-        to_frame(ob, yb, tile, y_s, y_r, j, twin).wait_recv()
-        beside = yb[tile].astype(F32)
-
-        @pl.when(has_prev)
-        def _():
-            to_frame(ps, pr, tile, z_s, z_r, j, frame - 2).wait_recv()
-
-        @pl.when(jnp.logical_not(has_prev))
-        def _():
-            pr[tile] = jnp.zeros(pr.shape[1:], BF16)
-
-        before = pr[tile].astype(F32)
-
-        @pl.when(has_next)
-        def _():
-            ps[tile] = (before + (st[tile] + beside)).astype(BF16)
-            to_frame(ps, pr, tile, z_s, z_r, j, frame + 2).start()
-
-        vb[tile] = (before + beside * odd.astype(F32) + st[tile]).astype(BF16)
-        to_other(vb, vb, tile, pv_s, pv_r, j).start()
 
     pairs = dim // PAIR
 
@@ -289,24 +297,38 @@
                 for copy in copies:
                     copy.wait_recv()
             realign(tokens, tokens + width, 0, pairs)
-        realign(0, tokens, 3 * stage, 3 * stage + 3)
-
-    stages = -(-pairs // 3)
-
-    @pl.when(has_prev)
+        realign(0, tokens, SHARE * stage, SHARE * (stage + 1))
+
+    stages = -(-pairs // SHARE)
+    deep = pair > 1
+
+    @pl.when(deep)
     def _():
         for stage in range(stages):
             prepare(stage)
 
     begun = 0
-    for j in range(steps + AHEAD):
-        if j < steps:
-            scan_step(j)
-        if j < stages:
+    for m in range(-max(FIRST, MIDDLE, LAST, stages), steps):
+        if steps - EARLY <= m + FIRST < steps:
             @pl.when(jnp.logical_not(has_prev))
             def _():
-                prepare(j)
-        m = j - AHEAD
+                scan_step(m + FIRST, True)
+
+        if 0 <= m + MIDDLE < steps:
+            @pl.when(jnp.logical_and(has_prev, has_next))
+            def _():
+                scan_step(m + MIDDLE, False)
+
+        if 0 <= m + LAST < steps:
+            @pl.when(jnp.logical_and(has_prev, jnp.logical_not(has_next)))
+            def _():
+                scan_step(m + LAST, False)
+
+        if 0 <= m + stages < stages:
+            @pl.when(jnp.logical_not(deep))
+            def _():
+                prepare(m + stages)
+
         if m < 0:
             continue
         to_other(vb, vb, 2 * m + other, pv_s, pv_r, m).wait_recv()
@@ -333,12 +355,14 @@
     def drain_step(j, _):
         mine, theirs = 2 * j + space, 2 * j + other
         to_other(pb, rb, theirs, rs_s, rs_r, j).wait_send()
-        to_frame(ob, yb, mine, y_s, y_r, j, twin).wait_send()
+        for half in range(2):
+            to_frame(ob, yb, mine, y_s, y_r, j, half, twin).wait_send()
         to_other(vb, vb, mine, pv_s, pv_r, j).wait_send()
 
         @pl.when(has_next)
         def _():
-            to_frame(ps, pr, mine, z_s, z_r, j, frame + 2).wait_send()
+            for half in range(2):
+                to_frame(ps, pr, mine, z_s, z_r, j, half, frame + 2).wait_send()
 
         return 0
 
@@ -392,7 +416,9 @@
                 pieces,
                 pieces,
             ]
-            + [sems] * 8
+            + [sems] * 2
+            + [pltpu.SemaphoreType.DMA((2, steps))] * 4
+            + [sems] * 2
             + [pltpu.SemaphoreType.DMA((3,))],
             compiler_params=pltpu.CompilerParams(collective_id=0, has_side_effects=True, vmem_limit_bytes=50 << 20),
         )(*(pltpu.with_memory_space_constraint(a, pltpu.HBM) for a in operands))

time: 30.5 us -> 30.3 us (level)
  no operation moved by 1% of the time
where the time goes in v4:
time: 30.3 us; the launch traced here: 30.2 us
  Pallas kernels  28.8 us (95%)
  local copies, waits for them, and re-layouts  1.36 us (4%)
    pallas_call x1, Pallas kernels, on_device(): pl.pallas_call(functools.partial(mix_kernel, frames, rows, width, dim), o...  28.8 us
    unnamed x1, local copies, waits for them, and re-layouts  1.36 us

profile of v4, /device:TPU:27, one launch (start us, length us, event | category | flops | bytes accessed | tf_op | source)
XLA Modules:
  0.0 30.2 jit_solution(3258501599710782517)
XLA Ops:
  0.0 28.8 %shard_map.73 = bf16[480,2240]{1,0:T(8,128)(2,1)S(1)} custom-call(bf16[480,2240]{1,0:T(8,128)(2,1)} %bitcast.6, bf16[480,2240]{1,0:T(8,128)(2,1)} %bitcast.7, bf16[480,2240]{1,0:T(8,128)(2,1)} %bitcast.8, bf16[480,2240]{1,0:T(8,128)(2,1)} %bitcast.9, f32[2240]{0:T(1024)} %gain_hbm.1, f32[9,2240]{1,0:T(8,128)} %vt_hbm.1, f32[9,2240]{1,0:T(8,128)} %gt_hbm.1), custom_call_target="tpu_custom_call" | custom-call | tf_op jit(solution)/shard_map/pallas_call | solution.py:388
  28.8 1.4 %copy.9 = bf16[1,6,80,2240]{3,2,1,0:T(8,128)(2,1)} copy(bf16[1,6,80,2240]{3,2,1,0:T(8,128)(2,1)S(1)} %bitcast.5) | data formatting | bytes 4300800

commit v5 on v4

--- a/solution.py
+++ b/solution.py
@@ -34,7 +34,7 @@
 def mix_kernel(
     frames, rows, width, dim,
     q_hbm, k_hbm, v_hbm, r_hbm, gain_hbm, vt_hbm, gt_hbm, o_ref,
-    q, k, v, kt, res, st, pb, rb, ob, yb, pr, ps, vb, qa, ra, gain_ref, ga, vt_ref, gt_ref, taps, numer, sq, mixed, x32,
+    q, k, v, kt, res, st, pb, rb, ob, yb, pr, ps, vb, qa, ra, gain_ref, ga, vt_ref, gt_ref, taps, numer, sq, mixed, x32, left, right,
     kv_sem, load_sem, edge_s, edge_r, rs_s, rs_r, y_s, y_r, z_s, z_r, pv_s, pv_r, small_sem,
 ):
     tokens = rows * width
@@ -92,10 +92,11 @@
     x32[...] = jnp.zeros(x32.shape, F32)
     taps[...] = jnp.zeros(taps.shape, F32)
     mixed[:, dim:] = jnp.zeros((mixed.shape[0], mixed.shape[1] - dim), BF16)
+    mixed[pl.ds(pl.multiple_of(space * (tokens + width), width), width), :] = jnp.zeros((width, mixed.shape[1]), BF16)
 
     def to_other(src, dst, tile, send, recv, j):
         return pltpu.make_async_remote_copy(
-            src_ref=src.at[tile], dst_ref=dst.at[tile], send_sem=send.at[j], recv_sem=recv.at[j],
+            src_ref=src.at[tile], dst_ref=dst.at[tile], send_sem=send.at[0], recv_sem=recv.at[j],
             device_id={"space": other},
         )
 
@@ -105,7 +106,7 @@
     def to_frame(src, dst, tile, send, recv, j, half, target):
         r0, r1 = halves[half]
         return pltpu.make_async_remote_copy(
-            src_ref=src.at[tile, r0:r1], dst_ref=dst.at[tile, r0:r1], send_sem=send.at[half, j], recv_sem=recv.at[half, j],
+            src_ref=src.at[tile, r0:r1], dst_ref=dst.at[tile, r0:r1], send_sem=send.at[0], recv_sem=recv.at[half, j],
             device_id={"frame": target},
         )
 
@@ -235,32 +236,44 @@
         for t in range(PAIR * j // LANES, done(j + 1)):
             lo, hi = LANES * t, min(dim, LANES * (t + 1))
             parts = [qa[n, :, a:b] for n, a, b in cover(lo, hi, PAIR)]
-            mixed[:, lo:hi] = jnp.concatenate(parts, axis=1) if len(parts) > 1 else parts[0]
+            value = jnp.concatenate(parts, axis=1) if len(parts) > 1 else parts[0]
+            mixed[width : width + tokens, lo:hi] = value[:tokens]
+            mixed[far, lo:hi] = value[tokens:]
 
     def done(j):
         return -(-dim // LANES) if j == pairs else PAIR * j // LANES
 
     pitch = width + 2 * PAD
-    far = pl.multiple_of((1 - space) * (rows + 1) * pitch + PAD, PAD)
+    far = pl.ds(pl.multiple_of((1 - space) * (tokens + width), width), width)
     chunk = 16
 
+    def tree(terms):
+        total = terms[0]
+        for term in terms[1:]:
+            total = total + term
+        return total
+
     def conv_tile(at, keep):
-        for row in range(rows):
-            first = (row + 1) * pitch + PAD
+        for row in range(rows + 2):
+            first = row * pitch + PAD
             x32[first : first + width, :] = mixed[row * width : (row + 1) * width, at].astype(F32)
-        x32[pl.ds(far, width), :] = mixed[tokens:, at].astype(F32)
-        tv = [jnp.broadcast_to(taps[0, n : n + 1, at], (chunk, LANES)) for n in range(9)]
-        tg = [jnp.broadcast_to(taps[1, n : n + 1, at], (chunk, LANES)) for n in range(9)]
+        for row in range(rows + 2):
+            first = row * pitch + PAD
+            here = slice(row * width, (row + 1) * width)
+            left[here, :] = x32[first - 1 : first - 1 + width, :].astype(BF16)
+            right[here, :] = x32[first + 1 : first + 1 + width, :].astype(BF16)
+        tv, tg = ([jnp.broadcast_to(taps[f, n : n + 1, at], (chunk, LANES)).astype(BF16) for n in range(9)] for f in range(2))
         for row in range(rows):
             for off in range(0, width, chunk):
-                cv, cg = None, None
+                cv = half = None
                 for n in range(9):
-                    start = (row + n // 3) * pitch + PAD - 1 + n % 3 + off
-                    x = x32[start : start + chunk, :]
+                    start = (row + n // 3) * width + off
+                    here = slice(start, start + chunk)
+                    x = left[here, :] if n % 3 == 0 else mixed[here, at] if n % 3 == 1 else right[here, :]
                     cv = tv[n] * x if cv is None else cv + tv[n] * x
-                    cg = tg[n] * x if cg is None else cg + tg[n] * x
+                    half = tg[n] * x if half is None else half + tg[n] * x
+                cv, half = cv.astype(F32), half.astype(F32)
                 centre = (row + 1) * pitch + PAD + off
-                half = 0.5 * cg
                 value = (x32[centre : centre + chunk, :] + cv * (half + half * jnp.tanh(half))).astype(BF16)
                 first = row * width + off
                 if keep == LANES:
@@ -283,7 +296,7 @@
     for copy in small:
         copy.wait()
     taps[0, 0:9, 0:dim] = vt_ref[...]
-    taps[1, 0:9, 0:dim] = gt_ref[...]
+    taps[1, 0:9, 0:dim] = 0.5 * gt_ref[...]
     for j in range(pairs):
         ga[j : j + 1, :PAIR] = gain_ref[PAIR * j : PAIR * (j + 1)].reshape(1, PAIR)
 
@@ -352,21 +365,18 @@
         for copy in copies:
             copy.wait_send()
 
-    def drain_step(j, _):
-        mine, theirs = 2 * j + space, 2 * j + other
-        to_other(pb, rb, theirs, rs_s, rs_r, j).wait_send()
-        for half in range(2):
-            to_frame(ob, yb, mine, y_s, y_r, j, half, twin).wait_send()
-        to_other(vb, vb, mine, pv_s, pv_r, j).wait_send()
-
-        @pl.when(has_next)
-        def _():
-            for half in range(2):
-                to_frame(ps, pr, mine, z_s, z_r, j, half, frame + 2).wait_send()
-
-        return 0
-
-    lax.fori_loop(0, steps, drain_step, 0)
+    def drain(buf, send, recv, target):
+        pltpu.make_async_remote_copy(
+            src_ref=buf.at[0:steps], dst_ref=buf.at[0:steps], send_sem=send.at[0], recv_sem=recv, device_id=target
+        ).wait_send()
+
+    drain(pb, rs_s, rs_r.at[0], {"space": other})
+    drain(ob, y_s, y_r.at[0, 0], {"frame": twin})
+    drain(vb, pv_s, pv_r.at[0], {"space": other})
+
+    @pl.when(has_next)
+    def _():
+        drain(ps, z_s, z_r.at[0, 0], {"frame": frame + 2})
 
 
 def solution(mesh):
@@ -379,7 +389,7 @@
         flat = lambda a: a.reshape(tokens, dim)
         anywhere = pl.BlockSpec(memory_space=pl.ANY)
         state = (2 * steps, HEAD_DIM, LANES)
-        sems = pltpu.SemaphoreType.DMA((steps,))
+        one, sems, split = (pltpu.SemaphoreType.DMA(n) for n in ((1,), (steps,), (2, steps)))
         pieces = pltpu.SemaphoreType.DMA((2, -(-dim // PIECE)))
         ext = tokens + width
         pairs = dim // PAIR
@@ -409,16 +419,16 @@
                 pltpu.VMEM((2, 16, across), F32),
                 pltpu.VMEM((2 * GROUP, ext, WINDOW), F32),
                 pltpu.VMEM((2 * GROUP, ext, WINDOW), BF16),
-                pltpu.VMEM((ext, across), BF16),
+                pltpu.VMEM((ext + width, across), BF16),
                 pltpu.VMEM(((rows + 2) * (width + 2 * PAD), LANES), F32),
+                pltpu.VMEM((ext + width, LANES), BF16),
+                pltpu.VMEM((ext + width, LANES), BF16),
                 pieces,
                 pieces,
                 pieces,
                 pieces,
             ]
-            + [sems] * 2
-            + [pltpu.SemaphoreType.DMA((2, steps))] * 4
-            + [sems] * 2
+            + [one, sems, one, split, one, split, one, sems]
             + [pltpu.SemaphoreType.DMA((3,))],
             compiler_params=pltpu.CompilerParams(collective_id=0, has_side_effects=True, vmem_limit_bytes=50 << 20),
         )(*(pltpu.with_memory_space_constraint(a, pltpu.HBM) for a in operands))

time: 30.3 us -> 27.8 us (0.917)
  Pallas kernels: 28.8 us -> 26.3 us
    pallas_call x1, Pallas kernels: 28.8 us -> 26.3 us  [on_device(): pl.pallas_call(functools.partial(mix_kernel, frames, rows, width, dim), o...]
where the time goes in v5:
time: 27.8 us; the launch traced here: 27.7 us
  Pallas kernels  26.3 us (95%)
  local copies, waits for them, and re-layouts  1.36 us (5%)
    pallas_call x1, Pallas kernels, on_device(): pl.pallas_call(functools.partial(mix_kernel, frames, rows, width, dim), o...  26.3 us
    unnamed x1, local copies, waits for them, and re-layouts  1.36 us

profile of v5, /device:TPU:27, one launch (start us, length us, event | category | flops | bytes accessed | tf_op | source)
XLA Modules:
  0.0 27.7 jit_solution(14361268164219678942)
XLA Ops:
  0.0 26.3 %shard_map.73 = bf16[480,2240]{1,0:T(8,128)(2,1)S(1)} custom-call(bf16[480,2240]{1,0:T(8,128)(2,1)} %bitcast.6, bf16[480,2240]{1,0:T(8,128)(2,1)} %bitcast.7, bf16[480,2240]{1,0:T(8,128)(2,1)} %bitcast.8, bf16[480,2240]{1,0:T(8,128)(2,1)} %bitcast.9, f32[2240]{0:T(1024)} %gain_hbm.1, f32[9,2240]{1,0:T(8,128)} %vt_hbm.1, f32[9,2240]{1,0:T(8,128)} %gt_hbm.1), custom_call_target="tpu_custom_call" | custom-call | tf_op jit(solution)/shard_map/pallas_call | solution.py:398
  26.3 1.4 %copy.9 = bf16[1,6,80,2240]{3,2,1,0:T(8,128)(2,1)} copy(bf16[1,6,80,2240]{3,2,1,0:T(8,128)(2,1)S(1)} %bitcast.5) | data formatting | bytes 4300800

commit v6 on v5

--- a/solution.py
+++ b/solution.py
@@ -18,6 +18,7 @@
 EARLY = 7
 SHARE = 4
 GROUP = 2
+SINGLES = 4
 FIRST, MIDDLE, LAST = 6, 4, 2
 F32, BF16 = jnp.float32, jnp.bfloat16
 
@@ -230,7 +231,7 @@
 
     def mixed_step(j):
         total = jnp.dot(sq[j % (2 * GROUP), :, :PAIR], same, preferred_element_type=F32)
-        scale = lax.rsqrt(total * (1.0 / HEAD_DIM) + 1e-6)
+        scale = lax.rsqrt(total + HEAD_DIM * 1e-6)
         normed = numer[j % (2 * GROUP), :, :PAIR] * scale
         qa[j, :, :PAIR] = (ra[j, :, :PAIR].astype(F32) + normed * ga[j : j + 1, :PAIR]).astype(BF16)
         for t in range(PAIR * j // LANES, done(j + 1)):
@@ -298,7 +299,7 @@
     taps[0, 0:9, 0:dim] = vt_ref[...]
     taps[1, 0:9, 0:dim] = 0.5 * gt_ref[...]
     for j in range(pairs):
-        ga[j : j + 1, :PAIR] = gain_ref[PAIR * j : PAIR * (j + 1)].reshape(1, PAIR)
+        ga[j : j + 1, :PAIR] = HEAD_DIM**0.5 * gain_ref[PAIR * j : PAIR * (j + 1)].reshape(1, PAIR)
 
     def prepare(stage):
         if stage == 0:
@@ -320,7 +321,11 @@
         for stage in range(stages):
             prepare(stage)
 
-    begun = 0
+    def reach(m):
+        return m + (LAST if m >= SINGLES - 1 else 1)
+
+    starts = list(range(SINGLES)) + list(range(SINGLES, pairs, GROUP)) + [pairs]
+    block = 0
     for m in range(-max(FIRST, MIDDLE, LAST, stages), steps):
         if steps - EARLY <= m + FIRST < steps:
             @pl.when(jnp.logical_not(has_prev))
@@ -332,10 +337,12 @@
             def _():
                 scan_step(m + MIDDLE, False)
 
-        if 0 <= m + LAST < steps:
+        ahead = range(max(0, reach(m - 1) + 1), min(steps - 1, reach(m)) + 1)
+        if len(ahead):
             @pl.when(jnp.logical_and(has_prev, jnp.logical_not(has_next)))
             def _():
-                scan_step(m + LAST, False)
+                for n in ahead:
+                    scan_step(n, False)
 
         if 0 <= m + stages < stages:
             @pl.when(jnp.logical_not(deep))
@@ -345,21 +352,17 @@
         if m < 0:
             continue
         to_other(vb, vb, 2 * m + other, pv_s, pv_r, m).wait_recv()
-        while begun < pairs:
-            until = min(pairs, begun + GROUP)
-            if (PAIR * until - 1) // WINDOW > m:
-                break
-            for n in range(begun, until):
+        while block + 1 < len(starts) and (PAIR * starts[block + 1] - 1) // WINDOW <= m:
+            for n in range(starts[block], starts[block + 1]):
                 numer_step(n)
-            for n in range(max(0, begun - GROUP), begun):
-                mixed_step(n)
-            if begun:
-                conv_step(done(max(0, begun - GROUP)), done(begun))
-            begun = until
-    last = (pairs - 1) // GROUP * GROUP
-    for n in range(last, pairs):
+            if block:
+                for n in range(starts[block - 1], starts[block]):
+                    mixed_step(n)
+                conv_step(done(starts[block - 1]), done(starts[block]))
+            block += 1
+    for n in range(starts[-2], pairs):
         mixed_step(n)
-    conv_step(done(last), done(pairs))
+    conv_step(done(starts[-2]), done(pairs))
 
     for copies in edges:
         for copy in copies:

time: 27.8 us -> 27 us (0.971); the launches traced: 27.7 us -> 26.5 us
  Pallas kernels: 26.3 us -> 25.2 us
    pallas_call x1, Pallas kernels: 26.3 us -> 25.2 us  [on_device(): pl.pallas_call(functools.partial(mix_kernel, frames, rows, width, dim), o...]
where the time goes in v6:
time: 27 us; the launch traced here: 26.5 us
  Pallas kernels  25.2 us (93%)
  local copies, waits for them, and re-layouts  1.36 us (5%)
    pallas_call x1, Pallas kernels, on_device(): pl.pallas_call(functools.partial(mix_kernel, frames, rows, width, dim), o...  25.2 us
    unnamed x1, local copies, waits for them, and re-layouts  1.36 us

profile of v6, /device:TPU:27, one launch (start us, length us, event | category | flops | bytes accessed | tf_op | source)
XLA Modules:
  0.0 26.5 jit_solution(12097285766147547236)
XLA Ops:
  0.0 25.2 %shard_map.73 = bf16[480,2240]{1,0:T(8,128)(2,1)S(1)} custom-call(bf16[480,2240]{1,0:T(8,128)(2,1)} %bitcast.6, bf16[480,2240]{1,0:T(8,128)(2,1)} %bitcast.7, bf16[480,2240]{1,0:T(8,128)(2,1)} %bitcast.8, bf16[480,2240]{1,0:T(8,128)(2,1)} %bitcast.9, f32[2240]{0:T(1024)} %gain_hbm.1, f32[9,2240]{1,0:T(8,128)} %vt_hbm.1, f32[9,2240]{1,0:T(8,128)} %gt_hbm.1), custom_call_target="tpu_custom_call" | custom-call | tf_op jit(solution)/shard_map/pallas_call | solution.py:401
  25.2 1.4 %copy.9 = bf16[1,6,80,2240]{3,2,1,0:T(8,128)(2,1)} copy(bf16[1,6,80,2240]{3,2,1,0:T(8,128)(2,1)S(1)} %bitcast.5) | data formatting | bytes 4300800

commit v7 on v6

--- a/solution.py
+++ b/solution.py
@@ -353,11 +353,12 @@
             continue
         to_other(vb, vb, 2 * m + other, pv_s, pv_r, m).wait_recv()
         while block + 1 < len(starts) and (PAIR * starts[block + 1] - 1) // WINDOW <= m:
+            if block:
+                for n in range(starts[block - 1], starts[block]):
+                    mixed_step(n)
             for n in range(starts[block], starts[block + 1]):
                 numer_step(n)
             if block:
-                for n in range(starts[block - 1], starts[block]):
-                    mixed_step(n)
                 conv_step(done(starts[block - 1]), done(starts[block]))
             block += 1
     for n in range(starts[-2], pairs):

time: 27 us -> 26.7 us (0.989)
  no operation moved by 1% of the time
where the time goes in v7:
time: 26.7 us; the launch traced here: 26.3 us
  Pallas kernels  25 us (94%)
  local copies, waits for them, and re-layouts  1.36 us (5%)
    pallas_call x1, Pallas kernels, on_device(): pl.pallas_call(functools.partial(mix_kernel, frames, rows, width, dim), o...  25 us
    unnamed x1, local copies, waits for them, and re-layouts  1.36 us

profile of v7, /device:TPU:27, one launch (start us, length us, event | category | flops | bytes accessed | tf_op | source)
XLA Modules:
  0.0 26.3 jit_solution(9869187287916049333)
XLA Ops:
  0.0 25.0 %shard_map.73 = bf16[480,2240]{1,0:T(8,128)(2,1)S(1)} custom-call(bf16[480,2240]{1,0:T(8,128)(2,1)} %bitcast.6, bf16[480,2240]{1,0:T(8,128)(2,1)} %bitcast.7, bf16[480,2240]{1,0:T(8,128)(2,1)} %bitcast.8, bf16[480,2240]{1,0:T(8,128)(2,1)} %bitcast.9, f32[2240]{0:T(1024)} %gain_hbm.1, f32[9,2240]{1,0:T(8,128)} %vt_hbm.1, f32[9,2240]{1,0:T(8,128)} %gt_hbm.1), custom_call_target="tpu_custom_call" | custom-call | tf_op jit(solution)/shard_map/pallas_call | solution.py:402
  25.0 1.4 %copy.9 = bf16[1,6,80,2240]{3,2,1,0:T(8,128)(2,1)} copy(bf16[1,6,80,2240]{3,2,1,0:T(8,128)(2,1)S(1)} %bitcast.5) | data formatting | bytes 4300800

commit v8 on v7

--- a/solution.py
+++ b/solution.py
@@ -227,7 +227,8 @@
         both = jnp.concatenate([jnp.where(first_head, slab, zero), jnp.where(first_head, zero, slab)], axis=0)
         found = jnp.dot(qa[j, :, :PAIR], both, preferred_element_type=F32)
         numer[j % (2 * GROUP), :, :PAIR] = found
-        sq[j % (2 * GROUP), :, :PAIR] = (found * found).astype(BF16)
+        near = found.astype(BF16)
+        sq[j % (2 * GROUP), :, :PAIR] = near * near
 
     def mixed_step(j):
         total = jnp.dot(sq[j % (2 * GROUP), :, :PAIR], same, preferred_element_type=F32)

time: 26.7 us -> 26.8 us (level)
  no operation moved by 1% of the time
where the time goes in v8:
time: 26.8 us; the launch traced here: 26.4 us
  Pallas kernels  25 us (93%)
  local copies, waits for them, and re-layouts  1.36 us (5%)
    pallas_call x1, Pallas kernels, on_device(): pl.pallas_call(functools.partial(mix_kernel, frames, rows, width, dim), o...  25 us
    unnamed x1, local copies, waits for them, and re-layouts  1.36 us

profile of v8, /device:TPU:27, one launch (start us, length us, event | category | flops | bytes accessed | tf_op | source)
XLA Modules:
  0.0 26.4 jit_solution(8686279097925835953)
XLA Ops:
  0.0 25.0 %shard_map.73 = bf16[480,2240]{1,0:T(8,128)(2,1)S(1)} custom-call(bf16[480,2240]{1,0:T(8,128)(2,1)} %bitcast.6, bf16[480,2240]{1,0:T(8,128)(2,1)} %bitcast.7, bf16[480,2240]{1,0:T(8,128)(2,1)} %bitcast.8, bf16[480,2240]{1,0:T(8,128)(2,1)} %bitcast.9, f32[2240]{0:T(1024)} %gain_hbm.1, f32[9,2240]{1,0:T(8,128)} %vt_hbm.1, f32[9,2240]{1,0:T(8,128)} %gt_hbm.1), custom_call_target="tpu_custom_call" | custom-call | tf_op jit(solution)/shard_map/pallas_call | solution.py:403
  25.0 1.4 %copy.9 = bf16[1,6,80,2240]{3,2,1,0:T(8,128)(2,1)} copy(bf16[1,6,80,2240]{3,2,1,0:T(8,128)(2,1)S(1)} %bitcast.5) | data formatting | bytes 4300800
